TPU v7x, 32 devices: a whole 2x2x4 slice. The times are simulated.
32 devices in a mesh: dp: 16 (over z, y, core), tile: 2 (over x).
Axes of the slice: x: 2, y: 2, z: 4, core: 2. Of those that a mesh axis runs over, the one named last changes fastest.
Arguments:
- tokens: bfloat16 [16, 1024, 768], P('dp', 'tile'), may hold values from -11 to 11
- segment_ids: int32 [16, 1024], P('dp'), may hold values from 0 to 7, never falling along the last dimension, each value on 1 to 256 neighbouring positions
- keep_mask: int32 [16, 1024], P('dp'), may hold values 0 or 1
- gain_one: float32 [768], replicated, may hold values from 0.25 to 1.75
- bias_one: float32 [768], replicated, may hold values from -3 to 3
- qkv_weight: bfloat16 [768, 2304], replicated, may hold values from -0.21875 to 0.21875
- query_bias: float32 [768], replicated, may hold values from -3 to 3
- value_bias: float32 [768], replicated, may hold values from -3 to 3
- out_weight: bfloat16 [768, 768], replicated, may hold values from -2 to 2
- out_bias: float32 [768], replicated, may hold values from -3 to 3
- gain_two: float32 [768], replicated, may hold values from 0.25 to 1.75
- bias_two: float32 [768], replicated, may hold values from -3 to 3
- fc1_weight: bfloat16 [768, 3072], replicated, may hold values from -0.21875 to 0.21875
- fc1_bias: float32 [3072], replicated, may hold values from -3 to 3
- fc2_weight: bfloat16 [3072, 768], replicated, may hold values from -0.15625 to 0.15625
- fc2_bias: float32 [768], replicated, may hold values from -3 to 3
- cotangent: bfloat16 [16, 1024, 768], P('dp', 'tile'), may hold values from -6 to 6
Outputs:
- output: bfloat16 [16, 1024, 768], P('dp', 'tile')
- grad_tokens: bfloat16 [16, 1024, 768], P('dp', 'tile')
- gain_one_grad: float32 [768], replicated
- bias_one_grad: float32 [768], replicated
- qkv_grad: float32 [768, 2304], P('dp', 'tile')
- query_bias_grad: float32 [768], replicated
- value_bias_grad: float32 [768], replicated
- out_grad: float32 [768, 768], P('dp', 'tile')
- out_bias_grad: float32 [768], replicated
- gain_two_grad: float32 [768], replicated
- bias_two_grad: float32 [768], replicated
- fc1_grad: float32 [768, 3072], P('dp', 'tile')
- fc1_bias_grad: float32 [3072], replicated
- fc2_grad: float32 [3072, 768], P('dp', 'tile')
- fc2_bias_grad: float32 [768], replicated
- root_mean: float32 [4], replicated
Inputs may be any that keep to these rules, and one draw needn't show every extreme that they name: `segment_ids`: within a sequence the ids never fall; each of the 8 images has 1 to 256 slots, and one has exactly 256.
All inputs are finite; a program needn't handle non-finite values. No bound on the sum of `keep_mask` on one device may be relied on, other than what follows from the above.
Results may differ from a plain program's by a relative error of at most 0.017.
Values may be sent and summed in bfloat16 or wider, within the bound.
A program may use at most 192 MiB of HBM per device.

v0:
```python
import jax
import jax.numpy as jnp
from jax import lax
from jax.sharding import PartitionSpec as P

HEAD_DIM = 64


def layer_norm(values, norm_gain, norm_bias):
    average = jnp.mean(values, axis=-1, keepdims=True)
    centred = values - average
    variance = jnp.mean(centred * centred, axis=-1, keepdims=True)
    return centred * lax.rsqrt(variance + 1e-06) * norm_gain + norm_bias


def exact_gelu(values):
    return jax.nn.gelu(values, approximate=False)


def on_device(
    tokens,
    segment_ids,
    keep_mask,
    gain_one,
    bias_one,
    qkv_weight,
    query_bias,
    value_bias,
    out_weight,
    out_bias,
    gain_two,
    bias_two,
    fc1_weight,
    fc1_bias,
    fc2_weight,
    fc2_bias,
    cotangent,
):
    sequences, tile_rows, model_width = tokens.shape
    length = segment_ids.shape[1]
    count_rows = sequences * tile_rows
    head_block = 4 * HEAD_DIM
    score_scale = HEAD_DIM ** (-0.5)
    offset = lax.axis_index("tile") * tile_rows
    query_ids = lax.dynamic_slice_in_dim(segment_ids, offset, tile_rows, 1)
    query_keep = lax.dynamic_slice_in_dim(keep_mask, offset, tile_rows, 1)
    positions = offset + jnp.arange(tile_rows, dtype=jnp.int32)
    key_places = jnp.arange(length, dtype=jnp.int32)
    own_slot = positions[:, None] == key_places[None, :]
    usable = (keep_mask[:, None, :] == 1) | own_slot[None]
    allowed = ((query_ids[:, :, None] == segment_ids[:, None, :]) & usable)[:, None]
    flattened = tokens.reshape(count_rows, model_width).astype(jnp.float32)
    normed = layer_norm(flattened, gain_one, bias_one)
    normed_low = normed.astype(jnp.bfloat16)
    key_bias = jnp.zeros_like(query_bias)
    projected = jnp.dot(
        normed_low, qkv_weight, preferred_element_type=jnp.float32
    ) + jnp.concatenate([query_bias, key_bias, value_bias])
    projected_low = projected.astype(jnp.bfloat16).reshape(sequences, tile_rows, 3 * model_width)
    queries = projected_low[..., :model_width]
    shared_local = projected_low[..., model_width:]
    shared_all = lax.all_gather(shared_local, "tile", axis=1, tiled=True)
    keys_all = shared_all[..., :model_width]
    values_all = shared_all[..., model_width:]
    key_count = shared_all.shape[1]

    def split_heads(source, column):
        sliced = source[..., column : column + head_block]
        return sliced.reshape(sliced.shape[0], sliced.shape[1], 4, HEAD_DIM)

    def block_scores(query_part, key_part):
        scores = (
            jnp.einsum("sqhe,skhe->shqk", query_part, key_part, preferred_element_type=jnp.float32)
            * score_scale
        )
        return jnp.where(allowed, scores, -1e30)

    attended_parts = []
    logsums = []
    for column in range(0, model_width, head_block):
        masked = block_scores(split_heads(queries, column), split_heads(keys_all, column))
        row_peak = jnp.max(masked, axis=-1, keepdims=True)
        exponent = jnp.exp(masked - row_peak)
        row_total = jnp.sum(exponent, axis=-1, keepdims=True)
        softmax_probs = (exponent / row_total).astype(jnp.bfloat16)
        logsums.append(row_peak + jnp.log(row_total))
        attended_parts.append(
            jnp.einsum(
                "shqk,skhe->sqhe",
                softmax_probs,
                split_heads(values_all, column),
                preferred_element_type=jnp.float32,
            )
        )
    attended = jnp.concatenate(attended_parts, axis=2)
    attended_low = attended.reshape(count_rows, model_width).astype(jnp.bfloat16)
    branch_one = jnp.dot(attended_low, out_weight, preferred_element_type=jnp.float32) + out_bias
    hidden = flattened + branch_one
    normed_two = layer_norm(hidden, gain_two, bias_two)
    normed_two_low = normed_two.astype(jnp.bfloat16)
    inner = jnp.dot(normed_two_low, fc1_weight, preferred_element_type=jnp.float32) + fc1_bias
    active_low = exact_gelu(inner).astype(jnp.bfloat16)
    branch_two = jnp.dot(active_low, fc2_weight, preferred_element_type=jnp.float32) + fc2_bias
    result = hidden + branch_two
    output = result.astype(jnp.bfloat16).reshape(sequences, tile_rows, model_width)
    weighting = query_keep.reshape(count_rows, 1).astype(jnp.float32)
    squares = [
        jnp.sum(weighting * member * member)
        for member in (flattened, branch_one, branch_two, result)
    ]
    stats = jnp.stack(squares + [jnp.sum(weighting)])
    grad_result = cotangent.reshape(count_rows, model_width)
    fc2_grad = jnp.einsum("nf,nd->fd", active_low, grad_result, preferred_element_type=jnp.float32)
    fc2_bias_grad = jnp.sum(grad_result.astype(jnp.float32), axis=0)
    grad_active = jnp.einsum(
        "nd,fd->nf", grad_result, fc2_weight, preferred_element_type=jnp.float32
    )
    inner_value, gelu_back = jax.vjp(exact_gelu, inner)
    grad_inner_low = gelu_back(grad_active)[0].astype(jnp.bfloat16)
    fc1_grad = jnp.einsum(
        "nd,nf->df", normed_two_low, grad_inner_low, preferred_element_type=jnp.float32
    )
    fc1_bias_grad = jnp.sum(grad_inner_low.astype(jnp.float32), axis=0)
    grad_normed_two = jnp.einsum(
        "nf,df->nd", grad_inner_low, fc1_weight, preferred_element_type=jnp.float32
    )
    normed_again, norm_back_two = jax.vjp(layer_norm, hidden, gain_two, bias_two)
    grad_hidden_part, gain_two_grad, bias_two_grad = norm_back_two(grad_normed_two)
    grad_hidden = grad_result.astype(jnp.float32) + grad_hidden_part
    grad_branch_low = grad_hidden.astype(jnp.bfloat16)
    out_grad = jnp.einsum(
        "nd,ne->de", attended_low, grad_branch_low, preferred_element_type=jnp.float32
    )
    out_bias_grad = jnp.sum(grad_branch_low.astype(jnp.float32), axis=0)
    grad_attended_low = (
        jnp.einsum("ne,de->nd", grad_branch_low, out_weight, preferred_element_type=jnp.float32)
        .astype(jnp.bfloat16)
        .reshape(sequences, tile_rows, model_width)
    )
    query_grads = []
    key_grads = []
    value_grads = []
    for block_index, column in enumerate(range(0, model_width, head_block)):
        query_part = split_heads(queries, column)
        key_part = split_heads(keys_all, column)
        value_part = split_heads(values_all, column)
        grad_part = split_heads(grad_attended_low, column)
        masked = block_scores(query_part, key_part)
        probs_again = jnp.exp(masked - logsums[block_index])
        grad_probs = jnp.einsum(
            "sqhe,skhe->shqk", grad_part, value_part, preferred_element_type=jnp.float32
        )
        centre = jnp.sum(probs_again * grad_probs, axis=-1, keepdims=True)
        grad_scores = (probs_again * (grad_probs - centre)).astype(jnp.bfloat16)
        query_grads.append(
            jnp.einsum("shqk,skhe->sqhe", grad_scores, key_part, preferred_element_type=jnp.float32)
            * score_scale
        )
        key_grads.append(
            jnp.einsum(
                "shqk,sqhe->skhe", grad_scores, query_part, preferred_element_type=jnp.float32
            )
            * score_scale
        )
        value_grads.append(
            jnp.einsum(
                "shqk,sqhe->skhe",
                probs_again.astype(jnp.bfloat16),
                grad_part,
                preferred_element_type=jnp.float32,
            )
        )
    grad_query = jnp.concatenate(query_grads, axis=2).reshape(sequences, tile_rows, model_width)
    grad_key_full = jnp.concatenate(key_grads, axis=2).reshape(sequences, key_count, model_width)
    grad_value_full = jnp.concatenate(value_grads, axis=2).reshape(
        sequences, key_count, model_width
    )
    grad_shared_full = jnp.concatenate([grad_key_full, grad_value_full], axis=-1)
    grad_shared = lax.psum_scatter(
        grad_shared_full.astype(jnp.bfloat16), "tile", scatter_dimension=1, tiled=True
    ).astype(jnp.float32)
    grad_projected_low = (
        jnp.concatenate([grad_query, grad_shared], axis=-1)
        .astype(jnp.bfloat16)
        .reshape(count_rows, 3 * model_width)
    )
    qkv_grad = jnp.einsum(
        "nd,ne->de", normed_low, grad_projected_low, preferred_element_type=jnp.float32
    )
    column_sums = jnp.sum(grad_projected_low.astype(jnp.float32), axis=0)
    query_bias_grad = column_sums[:model_width]
    value_bias_grad = column_sums[2 * model_width :]
    grad_normed = jnp.einsum(
        "ne,de->nd", grad_projected_low, qkv_weight, preferred_element_type=jnp.float32
    )
    normed_first, norm_back_one = jax.vjp(layer_norm, flattened, gain_one, bias_one)
    grad_tokens_part, gain_one_grad, bias_one_grad = norm_back_one(grad_normed)
    grad_tokens = (
        (grad_hidden + grad_tokens_part)
        .astype(jnp.bfloat16)
        .reshape(sequences, tile_rows, model_width)
    )
    totals_small = lax.psum(
        (
            gain_one_grad,
            bias_one_grad,
            query_bias_grad,
            value_bias_grad,
            out_bias_grad,
            gain_two_grad,
            bias_two_grad,
            fc1_bias_grad,
            fc2_bias_grad,
            stats,
        ),
        ("dp", "tile"),
    )
    matrices = (qkv_grad, out_grad, fc1_grad, fc2_grad)
    row_shares = (
        lax.psum_scatter(
            matrices[0].astype(jnp.bfloat16), "dp", scatter_dimension=0, tiled=True
        ).astype(jnp.float32),
        lax.psum_scatter(
            matrices[1].astype(jnp.bfloat16), "dp", scatter_dimension=0, tiled=True
        ).astype(jnp.float32),
        lax.psum_scatter(
            matrices[2].astype(jnp.bfloat16), "dp", scatter_dimension=0, tiled=True
        ).astype(jnp.float32),
        lax.psum_scatter(
            matrices[3].astype(jnp.bfloat16), "dp", scatter_dimension=0, tiled=True
        ).astype(jnp.float32),
    )
    reduced = (
        lax.psum_scatter(
            row_shares[0].astype(jnp.bfloat16), "tile", scatter_dimension=1, tiled=True
        ).astype(jnp.float32),
        lax.psum_scatter(
            row_shares[1].astype(jnp.bfloat16), "tile", scatter_dimension=1, tiled=True
        ).astype(jnp.float32),
        lax.psum_scatter(
            row_shares[2].astype(jnp.bfloat16), "tile", scatter_dimension=1, tiled=True
        ).astype(jnp.float32),
        lax.psum_scatter(
            row_shares[3].astype(jnp.bfloat16), "tile", scatter_dimension=1, tiled=True
        ).astype(jnp.float32),
    )
    totals = totals_small[9]
    root_mean = jnp.sqrt(totals[:4] / (totals[4] * model_width))
    return (
        output,
        grad_tokens,
        totals_small[0],
        totals_small[1],
        reduced[0],
        totals_small[2],
        totals_small[3],
        reduced[1],
        totals_small[4],
        totals_small[5],
        totals_small[6],
        reduced[2],
        totals_small[7],
        reduced[3],
        totals_small[8],
        root_mean,
    )


def solution(mesh):
    placed = (
        P("dp", "tile", None),
        P("dp", None),
        P("dp", None),
        P(),
        P(),
        P(),
        P(),
        P(),
        P(),
        P(),
        P(),
        P(),
        P(),
        P(),
        P(),
        P(),
        P("dp", "tile", None),
    )
    return jax.shard_map(
        on_device,
        mesh=mesh,
        in_specs=placed,
        out_specs=(
            P("dp", "tile", None),
            P("dp", "tile", None),
            P(),
            P(),
            P("dp", "tile"),
            P(),
            P(),
            P("dp", "tile"),
            P(),
            P(),
            P(),
            P("dp", "tile"),
            P(),
            P("dp", "tile"),
            P(),
            P(),
        ),
        check_vma=False,
    )
```

profile of v0, /device:TPU:0, one launch (start us, length us, event | category | flops | bytes accessed | tf_op | source)
XLA Modules:
  0.0 602.2 jit_solution(12091611203027383656)
XLA Ops:
  11.5 3.3 fusion.25
  17.7 2.0 fusion.106
  27.8 37.7 %all-gather.2.cloned.1.call-done = bf16[1,1024,1536]{2,1,0:T(8,128)(2,1)} async-done(((bf16[1,512,1536]{2,1,0:T(8,128)(2,1)}), bf16[1,1024,1536]{2,1,0:T(8,128)(2,1)}) %all-gather.2.cloned.1.call-update) | async-done | bytes 3145744 | tf_op jit(solution)/shard_map/all_gather | solution.py:62
  65.4 3.6 fusion.105
  69.0 2.0 copy.71
  71.0 2.1 copy.77
  73.1 2.0 copy.75
  75.1 2.0 copy.74
  77.2 2.1 copy.72
  79.2 2.1 copy.69
  81.3 3.1 fusion.110
  84.4 2.0 fusion.1
  86.5 2.1 fusion.80
  92.4 2.1 fusion.81
  99.6 2.1 fusion.79
  101.9 2.0 fusion.103
  104.3 21.1 %multiply_convert_fusion.3 = (bf16[512,3072]{1,0:T(8,128)(2,1)}, f32[512,3072]{1,0:T(8,128)}, f32[512,3072]{1,0:T(8,128)}) fusion(f32[3072]{0:T(1024)S(1)} %copy-done.61, bf16[768,3072]{1,0:T(8,128)(2,1)S(1)} %bitcast.237, f32[512,768]{1,0:T(8,128)S(1)} %get-tuple-element.48, f32[768]{0:T(1024)S(1)} %copy-done.63, f32[768]{0:T(1024)S(1)} %copy-done.58, ...), kind=kOutput, calls=%fused_computation.28 | convolution fusion | flops 2521694208 | bytes 22042624 | tf_op jit(solution)/shard_map/dot_general | solution.py:101
  125.4 8.6 %convert_reduce_fusion = (f32[3072]{0:T(1024)}, bf16[512,3072]{1,0:T(8,128)(2,1)S(1)}) fusion(f32[512,3072]{1,0:T(8,128)} %get-tuple-element.46, bf16[3072,768]{1,0:T(8,128)(2,1)S(1)} %bitcast.239, bf16[1,512,768]{2,1,0:T(8,128)(2,1)S(1)} %copy-done.23, f32[512,3072]{1,0:T(8,128)} %get-tuple-element.73, f32[3072]{0:T(1024)S(1)} %copy-done.61), kind=kOutput, calls=%fused_computation.26 | convolution fusion | flops 2442654720 | bytes 21258240 | tf_op jit(solution)/shard_map/nd,fd->nf/dot_general | solution.py:115
  134.0 2.7 fusion.112
  137.1 4.8 fusion.44
  147.3 2.3 fusion.57
  152.4 5.7 fusion.67
  158.1 7.0 %multiply_reduce_fusion.2 = (f32[4,512]{1,0:T(4,128)}, f32[4,512,1024]{2,1,0:T(8,128)}) fusion(f32[4,512,1024]{2,1,0:T(8,128)} %copy-done.3, f32[4,512]{1,0:T(4,128)S(1)} %copy-done.39, bf16[512,4,64]{0,2,1:T(8,128)(2,1)S(1)} %bitcast.212, bf16[1024,4,64]{0,2,1:T(8,128)(2,1)S(1)} %bitcast.223), kind=kOutput, calls=%fused_computation.8 | convolution fusion | flops 274724864 | bytes 17580032 | tf_op jit(solution)/shard_map/sqhe,skhe->shqk/dot_general | solution.py:150
  166.9 5.8 fusion.61
  172.7 7.2 %multiply_reduce_fusion = (f32[4,512]{1,0:T(4,128)}, f32[4,512,1024]{2,1,0:T(8,128)}) fusion(f32[4,512,1024]{2,1,0:T(8,128)} %copy-done.2, f32[4,512]{1,0:T(4,128)S(1)} %log_add_fusion, bf16[512,4,64]{0,2,1:T(8,128)(2,1)S(1)} %bitcast.214, bf16[1024,4,64]{0,2,1:T(8,128)(2,1)S(1)} %bitcast.221), kind=kOutput, calls=%fused_computation.2 | convolution fusion | flops 274724864 | bytes 17580032 | tf_op jit(solution)/shard_map/sqhe,skhe->shqk/dot_general | solution.py:150
  181.7 5.8 fusion.64
  187.6 7.0 %multiply_reduce_fusion.1 = (f32[4,512]{1,0:T(4,128)}, f32[4,512,1024]{2,1,0:T(8,128)}) fusion(f32[4,512,1024]{2,1,0:T(8,128)} %copy-done.1, f32[4,512]{1,0:T(4,128)S(1)} %log_add_fusion.1, bf16[512,4,64]{0,2,1:T(8,128)(2,1)S(1)} %bitcast.216, bf16[1024,4,64]{0,2,1:T(8,128)(2,1)S(1)} %bitcast.219), kind=kOutput, calls=%fused_computation.5 | convolution fusion | flops 274724864 | bytes 17580032 | tf_op jit(solution)/shard_map/sqhe,skhe->shqk/dot_general | solution.py:150
  194.7 7.0 %multiply_convert_fusion.2 = bf16[4,512,1024]{2,1,0:T(8,128)(2,1)S(1)} fusion(f32[4,512,1024]{2,1,0:T(8,128)} %get-tuple-element.79, f32[4,512,1024]{2,1,0:T(8,128)} %copy-done.3, f32[4,512]{1,0:T(4,128)} %get-tuple-element.78, f32[4,512]{1,0:T(4,128)} %log_add_fusion.2), kind=kLoop, calls=%fused_computation.7 | loop fusion | flops 8388608 | bytes 20987904 | tf_op jit(solution)/shard_map/convert_element_type | solution.py:154
  204.5 4.9 multiply_convert_fusion
  212.3 4.4 multiply_convert_fusion.1
  218.7 1.9 pad_maximum_fusion
  220.7 32.2 %reduce-scatter.20.cloned.1.call-done = bf16[48,768]{1,0:T(8,128)(2,1)} async-done(((bf16[768,768]{1,0:T(8,128)(2,1)}), bf16[48,768]{1,0:T(8,128)(2,1)}) %reduce-scatter.20.cloned.1.call-update) | async-done | bytes 73744 | tf_op jit(solution)/shard_map/reduce_scatter | solution.py:223
  254.7 7.2 %convolution_convert_fusion = bf16[3072,768]{1,0:T(8,128)(2,1)} fusion(bf16[512,3072]{1,0:T(8,128)(2,1)} %get-tuple-element.45, bf16[1,512,768]{2,1,0:T(8,128)(2,1)} %param.33), kind=kOutput, calls=%fused_computation.42 | convolution fusion | flops 2418278400 | bytes 8650752 | tf_op jit(solution)/shard_map/nf,nd->fd/dot_general | solution.py:113
  262.6 7.4 %convolution_convert_fusion.1 = bf16[768,3072]{1,0:T(8,128)(2,1)} fusion(bf16[512,3072]{1,0:T(8,128)(2,1)} %copy-done.66, f32[512,768]{1,0:T(8,128)} %copy-done.11, f32[768]{0:T(1024)S(1)} %copy-done.64, f32[768]{0:T(1024)S(1)} %copy-done.59, f32[512]{0:T(512)S(1)} %copy-done.56, f32[512]{0:T(512)S(1)} %copy-done.49), kind=kOutput, calls=%fused_computation.43 | convolution fusion | flops 2420244480 | bytes 9447424 | tf_op jit(solution)/shard_map/nd,nf->df/dot_general | solution.py:120
  270.1 3.9 fusion.78
  274.1 2.6 fusion.76
  279.1 18.5 %reduce-scatter.16.cloned.1.call-done = bf16[1,512,1536]{1,2,0:T(8,128)(2,1)} async-done(((bf16[1,1024,1536]{1,2,0:T(8,128)(2,1)}), bf16[1,512,1536]{1,2,0:T(8,128)(2,1)}) %reduce-scatter.16.cloned.1.call-update) | async-done | bytes 1572880 | tf_op jit(solution)/shard_map/reduce_scatter | solution.py:179
  297.5 6.0 convolution_convert_fusion.2
  303.6 7.7 %reduce-scatter.30.cloned.1.call-done = bf16[384,48]{1,0:T(8,128)(2,1)} async-done(((bf16[768,48]{1,0:T(8,128)(2,1)}), bf16[384,48]{1,0:T(8,128)(2,1)}) %reduce-scatter.30.cloned.1.call-update) | async-done | bytes 36880
  314.2 76.8 %reduce-scatter.26.cloned.1.call-done = bf16[192,768]{1,0:T(8,128)(2,1)} async-done(((bf16[3072,768]{1,0:T(8,128)(2,1)}), bf16[192,768]{1,0:T(8,128)(2,1)}) %reduce-scatter.26.cloned.1.call-update) | async-done | bytes 294928 | tf_op jit(solution)/shard_map/reduce_scatter | solution.py:229
  393.0 5.6 fusion.98
  401.2 68.2 %reduce-scatter.22.cloned.1.call-done = bf16[48,3072]{1,0:T(8,128)(2,1)} async-done(((bf16[768,3072]{1,0:T(8,128)(2,1)}), bf16[48,3072]{1,0:T(8,128)(2,1)}) %reduce-scatter.22.cloned.1.call-update) | async-done | bytes 294928 | tf_op jit(solution)/shard_map/reduce_scatter | solution.py:226
  469.7 2.0 convert_reduce_fusion.1
  471.7 3.8 stack.23
  476.1 4.8 convert_reduce_fusion.2
  480.9 59.9 %reduce-scatter.18.cloned.1.call-done = bf16[48,2304]{1,0:T(8,128)(2,1)} async-done(((bf16[768,2304]{1,0:T(8,128)(2,1)}), bf16[48,2304]{1,0:T(8,128)(2,1)}) %reduce-scatter.18.cloned.1.call-update) | async-done | bytes 221200 | tf_op jit(solution)/shard_map/reduce_scatter | solution.py:220
  540.9 2.0 copy.81
  543.5 41.5 %all-reduce = (f32[768]{0:T(1024)}, f32[768]{0:T(1024)}, f32[768]{0:T(1024)}, f32[768]{0:T(1024)}, f32[768]{0:T(1024)}, /*index=5*/f32[768]{0:T(1024)}, f32[768]...) all-reduce(f32[768]{0:T(1024)} %get-tuple-element.18, ...), channel_id=1, replica_groups=mesh['dp'=16,'tile'=2] {'dp','tile'}, use_global_device_ids=true, to_apply=%region_19.20 | all-reduce | flops 9221 | bytes 73768 | tf_op jit(solution)/shard_map/psum | solution.py:203
  (236 shorter events, 67.5 us)
Async XLA Ops:
  7.2 4.3 copy-start
  7.2 58.2 %all-gather.2.cloned.1.call-start = ((), (), s32[]{:S(2)}) async-start(), calls=%async_computation.9 | async-start | bytes 4718592 | tf_op jit(solution)/shard_map/all_gather | solution.py:62
  8.7 6.1 %copy-start.42 = (f32[512]{0:T(512)}, f32[512]{0:T(512)S(1)}, u32[]{:S(2)}) copy-start(f32[512]{0:T(512)S(1)} %broadcast_multiply_fusion.1) | copy-start | bytes 6148
  10.2 4.6 copy-start.45
  16.3 8.8 %copy-start.53 = (s32[1,1024]{1,0:T(1,128)S(1)}, s32[1,1024]{1,0:T(1,128)}, u32[]{:S(2)}) copy-start(s32[1,1024]{1,0:T(1,128)} %param.18) | copy-start | bytes 12292
  16.3 8.8 %copy-start.54 = (s32[1,1024]{1,0:T(1,128)S(1)}, s32[1,1024]{1,0:T(1,128)}, u32[]{:S(2)}) copy-start(s32[1,1024]{1,0:T(1,128)} %param.19) | copy-start | bytes 12292
  17.6 235.3 %reduce-scatter.20.cloned.1.call-start = ((), (), s32[]{:S(2)}) async-start(), calls=%async_computation.12 | async-start | bytes 1253376 | tf_op jit(solution)/shard_map/reduce_scatter | solution.py:223
  84.4 4.3 copy-start.1
  90.5 4.1 copy-start.2
  96.5 5.2 copy-start.3
  99.5 4.7 slice-start.4
  99.5 4.7 slice-start.5
  101.9 23.5 %slice-start.6 = ((s8[4718592]{0:T(1024)(128)(4,1)}), s8[4194304]{0:T(1024)(128)(4,1)S(1)}, s32[]{:S(2)}) async-start(s8[4718592]{0:T(1024)(128)(4,1)} %bitcast.238), calls=%async_computation.25 | async-start | bytes 8388608
  103.9 38.0 %copy-start.11 = (f32[512,768]{1,0:T(8,128)}, f32[512,768]{1,0:T(8,128)S(1)}, u32[]{:S(2)}) copy-start(f32[512,768]{1,0:T(8,128)S(1)} %get-tuple-element.48) | copy-start | bytes 4718596
  103.9 38.0 %copy-start.48 = (f32[512]{0:T(512)}, f32[512]{0:T(512)S(1)}, u32[]{:S(2)}) copy-start(f32[512]{0:T(512)S(1)} %broadcast_multiply_fusion) | copy-start | bytes 6148
  104.3 37.6 %copy-start.55 = (f32[512]{0:T(512)}, f32[512]{0:T(512)S(1)}, u32[]{:S(2)}) copy-start(f32[512]{0:T(512)S(1)} %fusion.91) | copy-start | bytes 6148
  104.3 21.1 %copy-start.23 = (bf16[1,512,768]{2,1,0:T(8,128)(2,1)S(1)}, bf16[1,512,768]{2,1,0:T(8,128)(2,1)}, u32[]{:S(2)}) copy-start(bf16[1,512,768]{2,1,0:T(8,128)(2,1)} %param.33) | copy-start | bytes 2359300
  104.3 21.1 %slice-start.7 = ((s8[4718592]{0:T(1024)(128)(4,1)}), s8[524288]{0:T(1024)(128)(4,1)S(1)}, s32[]{:S(2)}) async-start(s8[4718592]{0:T(1024)(128)(4,1)} %bitcast.238), calls=%async_computation.26 | async-start | bytes 1048576
  152.3 5.7 copy-start.24
  152.3 5.7 copy-start.33
  152.4 5.7 copy-start.39
  166.9 5.8 copy-start.25
  166.9 5.8 copy-start.31
  181.7 5.8 copy-start.26
  181.7 5.8 copy-start.29
  194.6 102.9 %reduce-scatter.16.cloned.1.call-start = ((), (), s32[]{:S(2)}) async-start(), calls=%async_computation.10 | async-start | bytes 4718592 | tf_op jit(solution)/shard_map/reduce_scatter | solution.py:179
  194.7 9.1 %slice-start.2 = ((s8[8388608]{0:T(1024)(128)(4,1)}), s8[4194304]{0:T(1024)(128)(4,1)S(1)}, s32[]{:S(2)}) async-start(s8[8388608]{0:T(1024)(128)(4,1)} %bitcast.190), calls=%async_computation.21 | async-start | bytes 8388608
  194.7 7.0 %copy-start.22 = (bf16[1,512,256]{1,2,0:T(8,128)(2,1)S(1)}, bf16[1,512,256]{1,2,0:T(8,128)(2,1)}, u32[]{:S(2)}) copy-start(bf16[1,512,256]{1,2,0:T(8,128)(2,1)} %copy.70) | copy-start | bytes 786436
  194.7 9.8 %slice-start.3 = ((s8[8388608]{0:T(1024)(128)(4,1)}), s8[4194304]{0:T(1024)(128)(4,1)S(1)}, s32[]{:S(2)}) async-start(s8[8388608]{0:T(1024)(128)(4,1)} %bitcast.190), calls=%async_computation.22 | async-start | bytes 8388608
  203.8 8.5 %slice-start = ((s8[8388608]{0:T(1024)(128)(4,1)}), s8[4194304]{0:T(1024)(128)(4,1)S(1)}, s32[]{:S(2)}) async-start(s8[8388608]{0:T(1024)(128)(4,1)} %bitcast.188), calls=%async_computation.19 | async-start | bytes 8388608
  204.5 4.9 copy-start.20
  204.5 7.8 %slice-start.1 = ((s8[8388608]{0:T(1024)(128)(4,1)}), s8[4194304]{0:T(1024)(128)(4,1)S(1)}, s32[]{:S(2)}) async-start(s8[8388608]{0:T(1024)(128)(4,1)} %bitcast.188), calls=%async_computation.20 | async-start | bytes 8388608
  212.3 4.4 copy-start.18
  220.7 90.6 %reduce-scatter.30.cloned.1.call-start = ((), (), s32[]{:S(2)}) async-start(), calls=%async_computation.17 | async-start | bytes 294912
  254.6 136.4 %reduce-scatter.26.cloned.1.call-start = ((), (), s32[]{:S(2)}) async-start(), calls=%async_computation.15 | async-start | bytes 5013504 | tf_op jit(solution)/shard_map/reduce_scatter | solution.py:229
  261.9 207.5 %reduce-scatter.22.cloned.1.call-start = ((), (), s32[]{:S(2)}) async-start(), calls=%async_computation.13 | async-start | bytes 5013504 | tf_op jit(solution)/shard_map/reduce_scatter | solution.py:226
  270.0 270.9 %reduce-scatter.18.cloned.1.call-start = ((), (), s32[]{:S(2)}) async-start(), calls=%async_computation.11 | async-start | bytes 3760128 | tf_op jit(solution)/shard_map/reduce_scatter | solution.py:220
  270.0 6.7 %copy-start.8 = (bf16[4,512,1024]{2,1,0:T(8,128)(2,1)S(1)}, bf16[4,512,1024]{2,1,0:T(8,128)(2,1)}, u32[]{:S(2)}) copy-start(bf16[4,512,1024]{2,1,0:T(8,128)(2,1)} %copy-done.7) | copy-start | bytes 12582916
  270.0 6.6 %copy-start.17 = (bf16[1,1024,256]{1,2,0:T(8,128)(2,1)S(1)}, bf16[1,1024,256]{1,2,0:T(8,128)(2,1)}, u32[]{:S(2)}) copy-start(bf16[1,1024,256]{1,2,0:T(8,128)(2,1)} %copy.74) | copy-start | bytes 1572868
  274.0 23.5 %copy-start.43 = (f32[512]{0:T(512)S(1)}, f32[512]{0:T(512)}, u32[]{:S(2)}) copy-start(f32[512]{0:T(512)} %copy-done.42) | copy-start | bytes 6148
  274.0 23.5 %copy-start.46 = (f32[512]{0:T(512)S(1)}, f32[512]{0:T(512)}, u32[]{:S(2)}) copy-start(f32[512]{0:T(512)} %copy-done.45) | copy-start | bytes 6148
  274.0 23.5 %copy-start.52 = (f32[768]{0:T(1024)S(1)}, f32[768]{0:T(1024)}, u32[]{:S(2)}) copy-start(f32[768]{0:T(1024)} %param.20) | copy-start | bytes 9220
  274.0 23.5 %copy-start.65 = (f32[768]{0:T(1024)S(1)}, f32[768]{0:T(1024)}, u32[]{:S(2)}) copy-start(f32[768]{0:T(1024)} %param.21) | copy-start | bytes 9220
  303.5 283.2 %reduce-scatter.32.cloned.1.call-start = ((), (), s32[]{:S(2)}) async-start(), calls=%async_computation.18 | async-start | bytes 589824
  392.9 197.2 %reduce-scatter.24.cloned.1.call-start = ((), (), s32[]{:S(2)}) async-start(), calls=%async_computation.14 | async-start | bytes 442368 | tf_op jit(solution)/shard_map/reduce_scatter | solution.py:240
  393.0 5.6 copy-start.51
  393.0 6.8 %copy-start.10 = (bf16[1,512,768]{2,1,0:T(8,128)(2,1)S(1)}, bf16[1,512,768]{2,1,0:T(8,128)(2,1)}, u32[]{:S(2)}) copy-start(bf16[1,512,768]{2,1,0:T(8,128)(2,1)} %param.17) | copy-start | bytes 2359300
  469.4 122.3 %reduce-scatter.28.cloned.1.call-start = ((), (), s32[]{:S(2)}) async-start(), calls=%async_computation.16 | async-start | bytes 884736
  (38 other events, 77.4 us)
Sparse Core Ops, SparseCore 0:
  17.8 47.6 all-gather.1
  194.7 58.1 reduce-scatter.19
  255.1 42.3 reduce-scatter.15
  300.3 10.9 reduce-scatter.29
  315.4 75.5 reduce-scatter.25
  394.7 74.5 reduce-scatter.21
  473.7 67.0 reduce-scatter.17
  543.2 12.3 reduce-scatter.31
  557.8 11.9 reduce-scatter.23
  571.9 15.7 reduce-scatter.27
where the time goes:
time: 609 us; the launch traced here: 602 us
  waiting for transfers between devices  301 us (49%)
  matrix products  135 us (22%)
  local copies, waits for them, and re-layouts  57.3 us (9%)
  other arithmetic  50.4 us (8%)
  blocking collectives  41.5 us (7%)
  between operations  16 us (3%)
    reduce_scatter x1, waiting for transfers between devices, on_device(): lax.psum_scatter(matrices[3].astype(jnp.bfloat16), 'dp', scatter_dimensio...  76.8 us
    reduce_scatter x1, waiting for transfers between devices, on_device(): lax.psum_scatter(matrices[2].astype(jnp.bfloat16), 'dp', scatter_dimensio...  68.2 us
    reduce_scatter x1, waiting for transfers between devices, on_device(): lax.psum_scatter(matrices[0].astype(jnp.bfloat16), 'dp', scatter_dimensio...  59.9 us
    psum x1, blocking collectives, on_device(): lax.psum((gain_one_grad, bias_one_grad, query_bias_grad, value_bias_grad,...  41.5 us
    all_gather x1, waiting for transfers between devices, on_device(): shared_all = lax.all_gather(shared_local, 'tile', axis=1, tiled=True)  37.7 us
    reduce_scatter x1, waiting for transfers between devices, on_device(): lax.psum_scatter(matrices[1].astype(jnp.bfloat16), 'dp', scatter_dimensio...  32.2 us
    slice x15, local copies, waits for them, and re-layouts, split_heads(): sliced = source[..., column:column + head_block]  29.6 us
    unnamed x158, local copies, waits for them, and re-layouts  21.5 us
  transfers between devices with their start and end apart: 10, of which 7 were waited for; matrix products, arithmetic and copies ran while one was open for 16% of the time, Pallas kernels for 0%

commit v1 on v0

--- a/solution.py
+++ b/solution.py
@@ -201,19 +201,22 @@
         .reshape(sequences, tile_rows, model_width)
     )
     totals_small = lax.psum(
-        (
-            gain_one_grad,
-            bias_one_grad,
-            query_bias_grad,
-            value_bias_grad,
-            out_bias_grad,
-            gain_two_grad,
-            bias_two_grad,
-            fc1_bias_grad,
-            fc2_bias_grad,
-            stats,
+        lax.psum(
+            (
+                gain_one_grad,
+                bias_one_grad,
+                query_bias_grad,
+                value_bias_grad,
+                out_bias_grad,
+                gain_two_grad,
+                bias_two_grad,
+                fc1_bias_grad,
+                fc2_bias_grad,
+                stats,
+            ),
+            "tile",
         ),
-        ("dp", "tile"),
+        "dp",
     )
     matrices = (qkv_grad, out_grad, fc1_grad, fc2_grad)
     row_shares = (

time: 609 us -> 637 us (1.046)
  blocking collectives: 41.5 us -> 69.4 us
    psum x0 -> x1, blocking collectives: none -> 58.8 us  [on_device(): lax.psum(lax.psum((gain_one_grad, bias_one_grad, query_bias_grad, value_b...]
    psum x1, blocking collectives: 41.5 us -> 10.6 us  [on_device(): lax.psum((gain_one_grad, bias_one_grad, query_bias_grad, value_bias_grad,...]
  transfers between devices with their start and end apart: 10 -> 10, of which waited for: 7 -> 7; matrix products, arithmetic and copies ran while one was open for 16% -> 15% of each run, Pallas kernels for 0% -> 0%
where the time goes in v1:
time: 637 us; the launch traced here: 630 us
  waiting for transfers between devices  301 us (47%)
  matrix products  135 us (21%)
  blocking collectives  69.4 us (11%)
  local copies, waits for them, and re-layouts  57.4 us (9%)
  other arithmetic  50.5 us (8%)
  between operations  16 us (3%)
    reduce_scatter x1, waiting for transfers between devices, on_device(): lax.psum_scatter(matrices[3].astype(jnp.bfloat16), 'dp', scatter_dimensio...  76.8 us
    reduce_scatter x1, waiting for transfers between devices, on_device(): lax.psum_scatter(matrices[2].astype(jnp.bfloat16), 'dp', scatter_dimensio...  68.2 us
    reduce_scatter x1, waiting for transfers between devices, on_device(): lax.psum_scatter(matrices[0].astype(jnp.bfloat16), 'dp', scatter_dimensio...  59.8 us
    psum x1, blocking collectives, on_device(): lax.psum(lax.psum((gain_one_grad, bias_one_grad, query_bias_grad, value_b...  58.8 us
    all_gather x1, waiting for transfers between devices, on_device(): shared_all = lax.all_gather(shared_local, 'tile', axis=1, tiled=True)  37.6 us
    reduce_scatter x1, waiting for transfers between devices, on_device(): lax.psum_scatter(matrices[1].astype(jnp.bfloat16), 'dp', scatter_dimensio...  32 us
    slice x15, local copies, waits for them, and re-layouts, split_heads(): sliced = source[..., column:column + head_block]  29.6 us
    unnamed x158, local copies, waits for them, and re-layouts  21.5 us
  transfers between devices with their start and end apart: 10, of which 7 were waited for; matrix products, arithmetic and copies ran while one was open for 15% of the time, Pallas kernels for 0%

profile of v1, /device:TPU:0, one launch (start us, length us, event | category | flops | bytes accessed | tf_op | source)
XLA Modules:
  0.0 629.9 jit_solution(2256394956460347064)
XLA Ops:
  11.5 3.3 fusion.25
  17.7 2.0 fusion.106
  27.8 37.6 %all-gather.2.cloned.1.call-done = bf16[1,1024,1536]{2,1,0:T(8,128)(2,1)} async-done(((bf16[1,512,1536]{2,1,0:T(8,128)(2,1)}), bf16[1,1024,1536]{2,1,0:T(8,128)(2,1)}) %all-gather.2.cloned.1.call-update) | async-done | bytes 3145744 | tf_op jit(solution)/shard_map/all_gather | solution.py:62
  65.4 3.5 fusion.105
  69.0 2.0 copy.71
  71.0 2.0 copy.77
  73.1 2.1 copy.75
  75.1 2.0 copy.74
  77.2 2.0 copy.72
  79.2 2.1 copy.69
  81.3 3.1 fusion.110
  84.4 2.0 fusion.1
  86.5 2.1 fusion.80
  92.4 2.1 fusion.81
  99.5 2.1 fusion.79
  101.9 2.0 fusion.103
  104.3 21.1 %multiply_convert_fusion.3 = (bf16[512,3072]{1,0:T(8,128)(2,1)}, f32[512,3072]{1,0:T(8,128)}, f32[512,3072]{1,0:T(8,128)}) fusion(f32[3072]{0:T(1024)S(1)} %copy-done.61, bf16[768,3072]{1,0:T(8,128)(2,1)S(1)} %bitcast.237, f32[512,768]{1,0:T(8,128)S(1)} %get-tuple-element.58, f32[768]{0:T(1024)S(1)} %copy-done.63, f32[768]{0:T(1024)S(1)} %copy-done.58, ...), kind=kOutput, calls=%fused_computation.28 | convolution fusion | flops 2521694208 | bytes 22042624 | tf_op jit(solution)/shard_map/dot_general | solution.py:101
  125.4 8.6 %convert_reduce_fusion = (f32[3072]{0:T(1024)}, bf16[512,3072]{1,0:T(8,128)(2,1)S(1)}) fusion(f32[512,3072]{1,0:T(8,128)} %get-tuple-element.56, bf16[3072,768]{1,0:T(8,128)(2,1)S(1)} %bitcast.239, bf16[1,512,768]{2,1,0:T(8,128)(2,1)S(1)} %copy-done.23, f32[512,3072]{1,0:T(8,128)} %get-tuple-element.83, f32[3072]{0:T(1024)S(1)} %copy-done.61), kind=kOutput, calls=%fused_computation.26 | convolution fusion | flops 2442654720 | bytes 21258240 | tf_op jit(solution)/shard_map/nd,fd->nf/dot_general | solution.py:115
  134.0 2.7 fusion.112
  137.1 4.8 fusion.44
  147.3 2.3 fusion.57
  152.3 5.7 fusion.67
  158.1 7.0 %multiply_reduce_fusion.2 = (f32[4,512]{1,0:T(4,128)}, f32[4,512,1024]{2,1,0:T(8,128)}) fusion(f32[4,512,1024]{2,1,0:T(8,128)} %copy-done.3, f32[4,512]{1,0:T(4,128)S(1)} %copy-done.39, bf16[512,4,64]{0,2,1:T(8,128)(2,1)S(1)} %bitcast.212, bf16[1024,4,64]{0,2,1:T(8,128)(2,1)S(1)} %bitcast.223), kind=kOutput, calls=%fused_computation.8 | convolution fusion | flops 274724864 | bytes 17580032 | tf_op jit(solution)/shard_map/sqhe,skhe->shqk/dot_general | solution.py:150
  166.9 5.8 fusion.61
  172.7 7.2 %multiply_reduce_fusion = (f32[4,512]{1,0:T(4,128)}, f32[4,512,1024]{2,1,0:T(8,128)}) fusion(f32[4,512,1024]{2,1,0:T(8,128)} %copy-done.2, f32[4,512]{1,0:T(4,128)S(1)} %log_add_fusion, bf16[512,4,64]{0,2,1:T(8,128)(2,1)S(1)} %bitcast.214, bf16[1024,4,64]{0,2,1:T(8,128)(2,1)S(1)} %bitcast.221), kind=kOutput, calls=%fused_computation.2 | convolution fusion | flops 274724864 | bytes 17580032 | tf_op jit(solution)/shard_map/sqhe,skhe->shqk/dot_general | solution.py:150
  181.7 5.8 fusion.64
  187.5 7.0 %multiply_reduce_fusion.1 = (f32[4,512]{1,0:T(4,128)}, f32[4,512,1024]{2,1,0:T(8,128)}) fusion(f32[4,512,1024]{2,1,0:T(8,128)} %copy-done.1, f32[4,512]{1,0:T(4,128)S(1)} %log_add_fusion.1, bf16[512,4,64]{0,2,1:T(8,128)(2,1)S(1)} %bitcast.216, bf16[1024,4,64]{0,2,1:T(8,128)(2,1)S(1)} %bitcast.219), kind=kOutput, calls=%fused_computation.5 | convolution fusion | flops 274724864 | bytes 17580032 | tf_op jit(solution)/shard_map/sqhe,skhe->shqk/dot_general | solution.py:150
  194.6 7.0 %multiply_convert_fusion.2 = bf16[4,512,1024]{2,1,0:T(8,128)(2,1)S(1)} fusion(f32[4,512,1024]{2,1,0:T(8,128)} %get-tuple-element.89, f32[4,512,1024]{2,1,0:T(8,128)} %copy-done.3, f32[4,512]{1,0:T(4,128)} %get-tuple-element.88, f32[4,512]{1,0:T(4,128)} %log_add_fusion.2), kind=kLoop, calls=%fused_computation.7 | loop fusion | flops 8388608 | bytes 20987904 | tf_op jit(solution)/shard_map/convert_element_type | solution.py:154
  204.5 4.9 multiply_convert_fusion
  212.3 4.4 multiply_convert_fusion.1
  220.7 32.0 %reduce-scatter.20.cloned.1.call-done = bf16[48,768]{1,0:T(8,128)(2,1)} async-done(((bf16[768,768]{1,0:T(8,128)(2,1)}), bf16[48,768]{1,0:T(8,128)(2,1)}) %reduce-scatter.20.cloned.1.call-update) | async-done | bytes 73744 | tf_op jit(solution)/shard_map/reduce_scatter | solution.py:226
  254.5 7.2 %convolution_convert_fusion = bf16[3072,768]{1,0:T(8,128)(2,1)} fusion(bf16[512,3072]{1,0:T(8,128)(2,1)} %get-tuple-element.55, bf16[1,512,768]{2,1,0:T(8,128)(2,1)} %param.33), kind=kOutput, calls=%fused_computation.42 | convolution fusion | flops 2418278400 | bytes 8650752 | tf_op jit(solution)/shard_map/nf,nd->fd/dot_general | solution.py:113
  262.4 7.4 %convolution_convert_fusion.1 = bf16[768,3072]{1,0:T(8,128)(2,1)} fusion(bf16[512,3072]{1,0:T(8,128)(2,1)} %copy-done.66, f32[512,768]{1,0:T(8,128)} %copy-done.11, f32[768]{0:T(1024)S(1)} %copy-done.64, f32[768]{0:T(1024)S(1)} %copy-done.59, f32[512]{0:T(512)S(1)} %copy-done.56, f32[512]{0:T(512)S(1)} %copy-done.49), kind=kOutput, calls=%fused_computation.43 | convolution fusion | flops 2420244480 | bytes 9447424 | tf_op jit(solution)/shard_map/nd,nf->df/dot_general | solution.py:120
  269.9 3.9 fusion.78
  273.9 2.6 fusion.76
  278.9 18.5 %reduce-scatter.16.cloned.1.call-done = bf16[1,512,1536]{1,2,0:T(8,128)(2,1)} async-done(((bf16[1,1024,1536]{1,2,0:T(8,128)(2,1)}), bf16[1,512,1536]{1,2,0:T(8,128)(2,1)}) %reduce-scatter.16.cloned.1.call-update) | async-done | bytes 1572880 | tf_op jit(solution)/shard_map/reduce_scatter | solution.py:179
  297.4 6.0 convolution_convert_fusion.2
  303.4 7.7 %reduce-scatter.30.cloned.1.call-done = bf16[384,48]{1,0:T(8,128)(2,1)} async-done(((bf16[768,48]{1,0:T(8,128)(2,1)}), bf16[384,48]{1,0:T(8,128)(2,1)}) %reduce-scatter.30.cloned.1.call-update) | async-done | bytes 36880
  314.1 76.8 %reduce-scatter.26.cloned.1.call-done = bf16[192,768]{1,0:T(8,128)(2,1)} async-done(((bf16[3072,768]{1,0:T(8,128)(2,1)}), bf16[192,768]{1,0:T(8,128)(2,1)}) %reduce-scatter.26.cloned.1.call-update) | async-done | bytes 294928 | tf_op jit(solution)/shard_map/reduce_scatter | solution.py:232
  392.8 5.6 fusion.98
  401.0 68.2 %reduce-scatter.22.cloned.1.call-done = bf16[48,3072]{1,0:T(8,128)(2,1)} async-done(((bf16[768,3072]{1,0:T(8,128)(2,1)}), bf16[48,3072]{1,0:T(8,128)(2,1)}) %reduce-scatter.22.cloned.1.call-update) | async-done | bytes 294928 | tf_op jit(solution)/shard_map/reduce_scatter | solution.py:229
  469.5 2.0 convert_reduce_fusion.1
  471.5 3.9 stack.23
  476.1 4.8 convert_reduce_fusion.2
  480.9 59.8 %reduce-scatter.18.cloned.1.call-done = bf16[48,2304]{1,0:T(8,128)(2,1)} async-done(((bf16[768,2304]{1,0:T(8,128)(2,1)}), bf16[48,2304]{1,0:T(8,128)(2,1)}) %reduce-scatter.18.cloned.1.call-update) | async-done | bytes 221200 | tf_op jit(solution)/shard_map/reduce_scatter | solution.py:223
  540.7 2.0 copy.81
  543.3 10.6 %all-reduce.1 = (f32[768]{0:T(1024)}, f32[768]{0:T(1024)}, f32[768]{0:T(1024)}, f32[768]{0:T(1024)}, f32[768]{0:T(1024)}, /*index=5*/f32[768]{0:T(1024)}, f32[76...) all-reduce(f32[768]{0:T(1024)} %get-tuple-element.18, ...), channel_id=1, replica_groups=mesh['dp'=16,'tile'=2] {'tile'}, use_global_device_ids=true, to_apply=%region_19.20 | all-reduce | flops 9221 | bytes 73768 | tf_op jit(solution)/shard_map/psum | solution.py:204
  553.9 58.8 %all-reduce = (f32[768]{0:T(1024)}, f32[768]{0:T(1024)}, f32[768]{0:T(1024)}, f32[768]{0:T(1024)}, f32[768]{0:T(1024)}, /*index=5*/f32[768]{0:T(1024)}, f32[768]...) all-reduce(f32[768]{0:T(1024)} %get-tuple-element.39, ...), channel_id=1, replica_groups=mesh['dp'=16,'tile'=2] {'dp'}, use_global_device_ids=true, to_apply=%region_20.21 | all-reduce | flops 9221 | bytes 73768 | tf_op jit(solution)/shard_map/psum | solution.py:203
  (237 shorter events, 69.5 us)
Async XLA Ops:
  7.2 4.3 copy-start
  7.2 58.2 %all-gather.2.cloned.1.call-start = ((), (), s32[]{:S(2)}) async-start(), calls=%async_computation.9 | async-start | bytes 4718592 | tf_op jit(solution)/shard_map/all_gather | solution.py:62
  8.7 6.1 copy-start.42
  10.2 4.6 copy-start.45
  16.3 8.8 %copy-start.53 = (s32[1,1024]{1,0:T(1,128)S(1)}, s32[1,1024]{1,0:T(1,128)}, u32[]{:S(2)}) copy-start(s32[1,1024]{1,0:T(1,128)} %param.18) | copy-start | bytes 12292
  16.3 8.8 %copy-start.54 = (s32[1,1024]{1,0:T(1,128)S(1)}, s32[1,1024]{1,0:T(1,128)}, u32[]{:S(2)}) copy-start(s32[1,1024]{1,0:T(1,128)} %param.19) | copy-start | bytes 12292
  17.6 235.1 %reduce-scatter.20.cloned.1.call-start = ((), (), s32[]{:S(2)}) async-start(), calls=%async_computation.12 | async-start | bytes 1253376 | tf_op jit(solution)/shard_map/reduce_scatter | solution.py:226
  84.4 4.3 copy-start.1
  90.5 4.1 copy-start.2
  96.4 5.3 copy-start.3
  99.5 4.7 slice-start.4
  99.5 4.7 slice-start.5
  101.9 23.5 %slice-start.6 = ((s8[4718592]{0:T(1024)(128)(4,1)}), s8[4194304]{0:T(1024)(128)(4,1)S(1)}, s32[]{:S(2)}) async-start(s8[4718592]{0:T(1024)(128)(4,1)} %bitcast.238), calls=%async_computation.25 | async-start | bytes 8388608
  103.9 38.0 %copy-start.11 = (f32[512,768]{1,0:T(8,128)}, f32[512,768]{1,0:T(8,128)S(1)}, u32[]{:S(2)}) copy-start(f32[512,768]{1,0:T(8,128)S(1)} %get-tuple-element.58) | copy-start | bytes 4718596
  103.9 38.0 %copy-start.48 = (f32[512]{0:T(512)}, f32[512]{0:T(512)S(1)}, u32[]{:S(2)}) copy-start(f32[512]{0:T(512)S(1)} %broadcast_multiply_fusion) | copy-start | bytes 6148
  104.3 37.7 %copy-start.55 = (f32[512]{0:T(512)}, f32[512]{0:T(512)S(1)}, u32[]{:S(2)}) copy-start(f32[512]{0:T(512)S(1)} %fusion.91) | copy-start | bytes 6148
  104.3 21.1 %copy-start.23 = (bf16[1,512,768]{2,1,0:T(8,128)(2,1)S(1)}, bf16[1,512,768]{2,1,0:T(8,128)(2,1)}, u32[]{:S(2)}) copy-start(bf16[1,512,768]{2,1,0:T(8,128)(2,1)} %param.33) | copy-start | bytes 2359300
  104.3 21.1 %slice-start.7 = ((s8[4718592]{0:T(1024)(128)(4,1)}), s8[524288]{0:T(1024)(128)(4,1)S(1)}, s32[]{:S(2)}) async-start(s8[4718592]{0:T(1024)(128)(4,1)} %bitcast.238), calls=%async_computation.26 | async-start | bytes 1048576
  152.3 5.7 copy-start.24
  152.3 5.7 copy-start.33
  152.3 5.7 copy-start.39
  166.9 5.8 copy-start.25
  166.9 5.8 copy-start.31
  181.7 5.8 copy-start.26
  181.7 5.8 copy-start.29
  194.6 102.8 %reduce-scatter.16.cloned.1.call-start = ((), (), s32[]{:S(2)}) async-start(), calls=%async_computation.10 | async-start | bytes 4718592 | tf_op jit(solution)/shard_map/reduce_scatter | solution.py:179
  194.6 9.1 %slice-start.2 = ((s8[8388608]{0:T(1024)(128)(4,1)}), s8[4194304]{0:T(1024)(128)(4,1)S(1)}, s32[]{:S(2)}) async-start(s8[8388608]{0:T(1024)(128)(4,1)} %bitcast.190), calls=%async_computation.21 | async-start | bytes 8388608
  194.6 7.0 %copy-start.22 = (bf16[1,512,256]{1,2,0:T(8,128)(2,1)S(1)}, bf16[1,512,256]{1,2,0:T(8,128)(2,1)}, u32[]{:S(2)}) copy-start(bf16[1,512,256]{1,2,0:T(8,128)(2,1)} %copy.70) | copy-start | bytes 786436
  194.6 9.8 %slice-start.3 = ((s8[8388608]{0:T(1024)(128)(4,1)}), s8[4194304]{0:T(1024)(128)(4,1)S(1)}, s32[]{:S(2)}) async-start(s8[8388608]{0:T(1024)(128)(4,1)} %bitcast.190), calls=%async_computation.22 | async-start | bytes 8388608
  203.7 8.5 %slice-start = ((s8[8388608]{0:T(1024)(128)(4,1)}), s8[4194304]{0:T(1024)(128)(4,1)S(1)}, s32[]{:S(2)}) async-start(s8[8388608]{0:T(1024)(128)(4,1)} %bitcast.188), calls=%async_computation.19 | async-start | bytes 8388608
  204.4 4.9 copy-start.20
  204.5 7.8 %slice-start.1 = ((s8[8388608]{0:T(1024)(128)(4,1)}), s8[4194304]{0:T(1024)(128)(4,1)S(1)}, s32[]{:S(2)}) async-start(s8[8388608]{0:T(1024)(128)(4,1)} %bitcast.188), calls=%async_computation.20 | async-start | bytes 8388608
  212.2 4.4 copy-start.18
  220.6 90.5 %reduce-scatter.30.cloned.1.call-start = ((), (), s32[]{:S(2)}) async-start(), calls=%async_computation.17 | async-start | bytes 294912
  254.4 136.4 %reduce-scatter.26.cloned.1.call-start = ((), (), s32[]{:S(2)}) async-start(), calls=%async_computation.15 | async-start | bytes 5013504 | tf_op jit(solution)/shard_map/reduce_scatter | solution.py:232
  261.7 207.4 %reduce-scatter.22.cloned.1.call-start = ((), (), s32[]{:S(2)}) async-start(), calls=%async_computation.13 | async-start | bytes 5013504 | tf_op jit(solution)/shard_map/reduce_scatter | solution.py:229
  269.8 270.9 %reduce-scatter.18.cloned.1.call-start = ((), (), s32[]{:S(2)}) async-start(), calls=%async_computation.11 | async-start | bytes 3760128 | tf_op jit(solution)/shard_map/reduce_scatter | solution.py:223
  269.9 6.7 %copy-start.8 = (bf16[4,512,1024]{2,1,0:T(8,128)(2,1)S(1)}, bf16[4,512,1024]{2,1,0:T(8,128)(2,1)}, u32[]{:S(2)}) copy-start(bf16[4,512,1024]{2,1,0:T(8,128)(2,1)} %copy-done.7) | copy-start | bytes 12582916
  269.9 6.6 %copy-start.17 = (bf16[1,1024,256]{1,2,0:T(8,128)(2,1)S(1)}, bf16[1,1024,256]{1,2,0:T(8,128)(2,1)}, u32[]{:S(2)}) copy-start(bf16[1,1024,256]{1,2,0:T(8,128)(2,1)} %copy.74) | copy-start | bytes 1572868
  273.8 23.5 %copy-start.43 = (f32[512]{0:T(512)S(1)}, f32[512]{0:T(512)}, u32[]{:S(2)}) copy-start(f32[512]{0:T(512)} %copy-done.42) | copy-start | bytes 6148
  273.9 23.5 %copy-start.46 = (f32[512]{0:T(512)S(1)}, f32[512]{0:T(512)}, u32[]{:S(2)}) copy-start(f32[512]{0:T(512)} %copy-done.45) | copy-start | bytes 6148
  273.9 23.5 %copy-start.52 = (f32[768]{0:T(1024)S(1)}, f32[768]{0:T(1024)}, u32[]{:S(2)}) copy-start(f32[768]{0:T(1024)} %param.20) | copy-start | bytes 9220
  273.9 23.5 %copy-start.65 = (f32[768]{0:T(1024)S(1)}, f32[768]{0:T(1024)}, u32[]{:S(2)}) copy-start(f32[768]{0:T(1024)} %param.21) | copy-start | bytes 9220
  303.4 311.1 %reduce-scatter.32.cloned.1.call-start = ((), (), s32[]{:S(2)}) async-start(), calls=%async_computation.18 | async-start | bytes 589824
  392.8 225.1 %reduce-scatter.24.cloned.1.call-start = ((), (), s32[]{:S(2)}) async-start(), calls=%async_computation.14 | async-start | bytes 442368 | tf_op jit(solution)/shard_map/reduce_scatter | solution.py:243
  392.8 5.6 copy-start.51
  392.8 6.8 %copy-start.10 = (bf16[1,512,768]{2,1,0:T(8,128)(2,1)S(1)}, bf16[1,512,768]{2,1,0:T(8,128)(2,1)}, u32[]{:S(2)}) copy-start(bf16[1,512,768]{2,1,0:T(8,128)(2,1)} %param.17) | copy-start | bytes 2359300
  469.2 150.3 %reduce-scatter.28.cloned.1.call-start = ((), (), s32[]{:S(2)}) async-start(), calls=%async_computation.16 | async-start | bytes 884736
  (38 other events, 77.4 us)
Sparse Core Ops, SparseCore 0:
  17.8 47.6 all-gather.1
  194.7 57.9 reduce-scatter.19
  254.9 42.3 reduce-scatter.15
  300.1 10.9 reduce-scatter.29
  315.3 75.5 reduce-scatter.25
  394.6 74.5 reduce-scatter.21
  473.5 67.0 reduce-scatter.17
  543.0 12.1 reduce-scatter.31
  557.4 12.0 reduce-scatter.23
  571.6 15.2 reduce-scatter.27
